TPU v7x, 128 devices: a whole 4x4x4 slice. The times are simulated.
128 devices in a mesh: batch: 8 (over x, core), item: 16 (over z, y).
Axes of the slice: x: 4, y: 4, z: 4, core: 2. Of those that a mesh axis runs over, the one named last changes fastest.
Arguments:
- user_vectors: bfloat16 [32768, 512], P(('batch', 'item')), may hold values from -6 to 6
- item_table: bfloat16 [524288, 512], P(('batch', 'item')), may hold values from -0.25 to 0.25
- tower_weight: bfloat16 [512, 512], replicated, may hold values from -3 to 3
- item_owner: int32 [32768, 1], P(('batch', 'item')), may hold values from 0 to 127; in each aligned block of 256 rows (0 to 255, 256 to 511, ...) at most 4 rows name the same one
- item_row: int32 [32768], P(('batch', 'item')), may hold values from 0 to 4095
Outputs:
- table_grad: bfloat16 [524288, 512], P(('batch', 'item'))
- weight_grad: float32 [512, 512], P(('batch', 'item'))
Inputs may be any that keep to these rules, and one draw needn't show every extreme that they name: `item_owner`: within the rows of one device (aligned blocks of 256 rows) no owner is named by more than 4 rows, a bound that some block reaches.
All inputs are finite; a program needn't handle non-finite values.
Results may differ from a plain program's by a relative error of at most 0.0075.
Values may be sent and summed in bfloat16 or wider, within the bound.
A program may use at most 64 MiB of HBM per device.

v0:
```python
import jax
import jax.numpy as jnp
from jax import lax
from jax.sharding import PartitionSpec as P

epsilon = 1e-06
score_scale = 60.0
cauchy_scale = 4.0


def local(user_vectors, item_table, tower_weight, item_owner, item_row):
    b_dev, width = user_vectors.shape
    n_batch = lax.axis_size("batch")
    n_item = lax.axis_size("item")
    devices = n_batch * n_item
    slots = 2 * b_dev // devices
    owner = item_owner[:, 0]
    onehot = (owner[:, None] == jnp.arange(devices, dtype=jnp.int32)[None, :]).astype(jnp.int32)
    rank = jnp.sum(jnp.cumsum(onehot, axis=0) * onehot, axis=1) - 1
    place = owner * slots + rank
    request = (
        jnp.zeros((devices * slots,), jnp.int32).at[place].set(item_row).reshape(devices, slots)
    )
    asked = lax.all_to_all(request, ("batch", "item"), split_axis=0, concat_axis=0, tiled=True)
    found = item_table[asked]
    back = lax.all_to_all(found, ("batch", "item"), split_axis=0, concat_axis=0, tiled=True)
    fetched, asked = (back, asked)
    embed = fetched.reshape(devices * slots, width)[place]
    hidden = jnp.dot(embed, tower_weight, preferred_element_type=jnp.float32)
    rscale = lax.rsqrt(jnp.mean(hidden * hidden, axis=1, keepdims=True) + epsilon)
    item_vec = (hidden * rscale / jnp.sqrt(jnp.float32(width))).astype(jnp.bfloat16)
    user_f = user_vectors.astype(jnp.float32)
    user_unit = (
        user_f
        * lax.rsqrt(jnp.mean(user_f * user_f, axis=1, keepdims=True) + epsilon)
        / jnp.sqrt(jnp.float32(width))
    ).astype(jnp.bfloat16)
    piece = lax.all_gather(user_unit, "batch", axis=0, tiled=True)
    score = (
        lax.dot_general(
            item_vec, piece, (((1,), (1,)), ((), ())), preferred_element_type=jnp.float32
        )
        * score_scale
    )
    expo = jnp.exp(score)
    partial_mix = jnp.dot(expo.astype(jnp.bfloat16), piece, preferred_element_type=jnp.float32)
    total = jnp.sum(expo, axis=1)
    unit_f = user_unit.astype(jnp.float32)
    positive = jnp.sum(item_vec.astype(jnp.float32) * unit_f, axis=1) * score_scale
    xent = jnp.log(total) - positive
    cweight = 1.0 / (1.0 + xent / cauchy_scale)
    dvec = cweight[:, None] * score_scale * (partial_mix / total[:, None] - unit_f)
    inner = jnp.sum(hidden * dvec, axis=1, keepdims=True)
    dhidden = (
        rscale / jnp.sqrt(jnp.float32(width)) * (dvec - hidden * rscale * rscale * inner / width)
    ).astype(jnp.bfloat16)
    weight_grad = lax.psum_scatter(
        lax.dot_general(
            embed, dhidden, (((0,), (0,)), ((), ())), preferred_element_type=jnp.float32
        ),
        ("batch", "item"),
        scatter_dimension=0,
        tiled=True,
    )
    drow = jnp.dot(dhidden, tower_weight.T, preferred_element_type=jnp.float32)
    outgoing = jnp.zeros((devices * slots, width), jnp.float32).at[place].set(drow)
    incoming = lax.all_to_all(
        outgoing.reshape(devices, slots, width).astype(jnp.bfloat16),
        ("batch", "item"),
        split_axis=0,
        concat_axis=0,
        tiled=True,
    ).astype(jnp.float32)
    arrived = incoming.reshape(devices * slots, width)
    table_grad = (
        jnp.zeros((item_table.shape[0], width), jnp.float32).at[asked.reshape(-1)].add(arrived)
    )
    return (table_grad.astype(jnp.bfloat16), weight_grad)


def solution(mesh):
    return jax.shard_map(
        local,
        mesh=mesh,
        in_specs=(
            P(("batch", "item"), None),
            P(("batch", "item"), None),
            P(),
            P(("batch", "item"), None),
            P(("batch", "item")),
        ),
        out_specs=(P(("batch", "item"), None), P(("batch", "item"), None)),
        check_vma=False,
    )
```

profile of v0, /device:TPU:1, one launch (start us, length us, event | category | flops | bytes accessed | tf_op | source)
XLA Modules:
  0.0 245.3 jit_solution(17994513546542418527)
XLA Ops:
  7.2 0.0 copy-start
  7.2 0.8 copy.10
  8.0 0.2 fusion.12
  8.3 0.9 fusion.13
  9.2 0.7 compare_select_fusion.2
  9.9 1.6 scatter_custom_fusion
  11.4 0.1 all_to_all.14
  11.6 21.1 %all_to_all.22 = s32[128,1,4]{2,1,0:T(1,128)S(1)} all-to-all(s32[128,1,4]{2,1,0:T(1,128)S(1)} %bitcast.34), channel_id=1, replica_groups=mesh['batch'=8,'item'=16] {'batch','item'}, dimensions={0} | all-to-all | bytes 4096 | tf_op jit(solution)/shard_map/all_to_all | solution.py:24
  32.7 0.1 reshape.147
  32.8 4.7 %gather_fusion = bf16[512,512]{1,0:T(8,128)(2,1)S(1)} fusion(bf16[4096,512]{1,0:T(8,128)(2,1)} %param.6, s32[1024]{0:T(1024)S(1)} %pad_clamp_fusion.1), kind=kCustom, calls=%fused_computation | custom fusion | bytes 1050624 | tf_op jit(solution)/shard_map/gather | solution.py:25
  37.5 0.0 copy-start.1
  37.5 0.9 reshape.146
  38.4 4.3 %all-to-all-start.1 = ((bf16[128,4,512]{2,1,0:T(4,128)(2,1)}), bf16[128,4,512]{2,1,0:T(4,128)(2,1)S(1)}, u32[]{:S(2)}, u32[]{:S(2)}) async-start(bf16[128,4,512]{2,1,0:T(4,128)(2,1)} %reshape.146), calls=%async_computation.1 | async-start | bytes 1048576 | tf_op jit(solution)/shard_map/all_to_all | solution.py:26
  42.7 0.0 all-gather.2.cloned.1.call-start
  42.8 0.0 copy-done.1
  42.8 0.1 fusion.6
  42.9 13.9 %all-to-all-done.1 = bf16[128,4,512]{2,1,0:T(4,128)(2,1)S(1)} async-done(((bf16[128,4,512]{2,1,0:T(4,128)(2,1)}), bf16[128,4,512]{2,1,0:T(4,128)(2,1)S(1)}, u32[]{:S(2)}, u32[]{:S(2)}) %all-to-all-start.1) | async-done | bytes 524320 | tf_op jit(solution)/shard_map/all_to_all | solution.py:26
  56.8 0.1 reshape.140
  57.0 1.2 gather_fusion.1
  58.1 0.0 copy-done
  58.1 0.4 multiply_reduce_fusion.1
  58.5 0.9 fusion.9
  59.4 0.0 all-gather.2.cloned.1.call-update
  59.4 0.0 copy-start.2
  59.5 0.0 all-reduce.3.cloned.1.call-start
  59.5 21.4 %all-gather.2.cloned.1.call-done = bf16[2048,512]{1,0:T(8,128)(2,1)} async-done(((bf16[256,512]{1,0:T(8,128)(2,1)}), bf16[2048,512]{1,0:T(8,128)(2,1)}) %all-gather.2.cloned.1.call-update) | async-done | bytes 2097168 | tf_op jit(solution)/shard_map/all_gather | solution.py:38
  80.9 0.0 copy-start.3
  80.9 2.6 %fusion.19 = (f32[256]{0:T(256)S(1)}, bf16[256,2048]{1,0:T(8,128)(2,1)S(1)}) fusion(bf16[2048,512]{1,0:T(8,128)(2,1)} %all-gather.2.cloned.1.call-done, f32[256,512]{1,0:T(8,128)S(1)} %get-tuple-element.7, f32[256]{0:T(256)S(1)} %get-tuple-element.5), kind=kOutput, calls=%fused_computation.48 | convolution fusion | flops 538836736 | bytes 3672064 | tf_op jit(solution)/shard_map/dot_general | solution.py:40
  83.6 0.0 copy-done.2
  83.6 0.0 copy-done.3
  83.6 0.8 multiply_reduce_fusion
  84.4 0.2 multiply_convert_fusion
  84.6 1.3 fusion.21
  85.9 0.0 all-reduce.3.cloned.1.call-update
  85.9 0.3 fusion.20
  86.3 1.7 scatter_custom_fusion.1
  88.0 0.1 convert_element_type.44
  88.0 0.9 convert_element_type.45
  88.9 8.3 %all-to-all-start.2 = ((bf16[128,4,512]{2,1,0:T(4,128)(2,1)}), bf16[128,4,512]{2,1,0:T(4,128)(2,1)S(1)}, u32[]{:S(2)}, u32[]{:S(2)}) async-start(bf16[128,4,512]{2,1,0:T(4,128)(2,1)} %convert_element_type.45), calls=%async_computation.2 | async-start | bytes 1048576 | tf_op jit(solution)/shard_map/all_to_all | solution.py:67
  97.3 0.5 broadcast.185
  97.8 0.8 reduce.3
  98.6 0.1 reshape.139
  98.7 12.9 %all-to-all-done.2 = bf16[128,4,512]{2,1,0:T(4,128)(2,1)S(1)} async-done(((bf16[128,4,512]{2,1,0:T(4,128)(2,1)}), bf16[128,4,512]{2,1,0:T(4,128)(2,1)S(1)}, u32[]{:S(2)}, u32[]{:S(2)}) %all-to-all-start.2) | async-done | bytes 524320 | tf_op jit(solution)/shard_map/all_to_all | solution.py:67
  111.6 0.1 reshape.181
  111.7 7.3 %scatter_custom_fusion.2 = f32[4096,512]{1,0:T(8,128)} fusion(s32[512]{0:T(512)S(1)} %bitcast.42, f32[512,512]{1,0:T(8,128)S(1)} %reshape.181, f32[]{:T(128)} %constant.12.clone.1), kind=kCustom, calls=%fused_computation.5 | custom fusion | flops 262144 | bytes 8388612 | tf_op jit(solution)/shard_map/scatter-add | solution.py:76
  119.0 6.0 %convert_element_type.46 = bf16[4096,512]{1,0:T(8,128)(2,1)} convert(f32[4096,512]{1,0:T(8,128)} %scatter_custom_fusion.2) | non-fusion elementwise | flops 2097152 | bytes 12582912 | tf_op jit(solution)/shard_map/convert_element_type | solution.py:78
  125.0 112.2 %all-reduce.3.cloned.1.call-done = f32[512,512]{1,0:T(8,128)} async-done(((f32[512,512]{1,0:T(8,128)}), f32[512,512]{1,0:T(8,128)}) %all-reduce.3.cloned.1.call-update) | async-done | bytes 1048592
  237.2 1.3 constant_dynamic-slice_fusion
  (13 shorter events, 0.1 us)
Async XLA Ops:
  7.2 50.9 %copy-start = (bf16[512,512]{1,0:T(8,128)(2,1)S(1)}, bf16[512,512]{1,0:T(8,128)(2,1)}, u32[]{:S(2)}) copy-start(bf16[512,512]{1,0:T(8,128)(2,1)} %param.7) | copy-start | bytes 1572868
  37.5 5.3 %copy-start.1 = (bf16[256,512]{1,0:T(8,128)(2,1)S(1)}, bf16[256,512]{1,0:T(8,128)(2,1)}, u32[]{:S(2)}) copy-start(bf16[256,512]{1,0:T(8,128)(2,1)} %param.5) | copy-start | bytes 786436
  38.4 18.4 %all-to-all-start.1 = ((bf16[128,4,512]{2,1,0:T(4,128)(2,1)}), bf16[128,4,512]{2,1,0:T(4,128)(2,1)S(1)}, u32[]{:S(2)}, u32[]{:S(2)}) async-start(bf16[128,4,512]{2,1,0:T(4,128)(2,1)} %reshape.146), calls=%async_computation.1 | async-start | bytes 1048576 | tf_op jit(solution)/shard_map/all_to_all | solution.py:26
  42.7 38.2 %all-gather.2.cloned.1.call-start = ((), (), s32[]{:S(2)}) async-start(), calls=%async_computation.3 | async-start | bytes 2359296 | tf_op jit(solution)/shard_map/all_gather | solution.py:38
  59.4 24.1 %copy-start.2 = (bf16[256,512]{1,0:T(8,128)(2,1)S(1)}, bf16[256,512]{1,0:T(8,128)(2,1)}, u32[]{:S(2)}) copy-start(bf16[256,512]{1,0:T(8,128)(2,1)} %get-tuple-element.3) | copy-start | bytes 786436
  59.5 177.7 %all-reduce.3.cloned.1.call-start = ((), (), s32[]{:S(2)}) async-start(), calls=%async_computation.4 | async-start | bytes 2097152
  80.9 2.6 %copy-start.3 = (bf16[2048,512]{1,0:T(8,128)(2,1)S(1)}, bf16[2048,512]{1,0:T(8,128)(2,1)}, u32[]{:S(2)}) copy-start(bf16[2048,512]{1,0:T(8,128)(2,1)} %all-gather.2.cloned.1.call-done) | copy-start | bytes 6291460
  88.9 22.7 %all-to-all-start.2 = ((bf16[128,4,512]{2,1,0:T(4,128)(2,1)}), bf16[128,4,512]{2,1,0:T(4,128)(2,1)S(1)}, u32[]{:S(2)}, u32[]{:S(2)}) async-start(bf16[128,4,512]{2,1,0:T(4,128)(2,1)} %convert_element_type.45), calls=%async_computation.2 | async-start | bytes 1048576 | tf_op jit(solution)/shard_map/all_to_all | solution.py:67
Sparse Core Ops, SparseCore 0:
  59.6 21.3 all-gather.1
  86.1 151.0 all-reduce.2
where the time goes:
time: 246 us; the launch traced here: 245 us
  waiting for transfers between devices  160 us (65%)
  blocking collectives  21.1 us (9%)
  other arithmetic  17.2 us (7%)
  between operations  14.3 us (6%)
  local copies, waits for them, and re-layouts  14.2 us (6%)
  starting transfers between devices  12.7 us (5%)
  matrix products  5.44 us (2%)
    unnamed x3, waiting for transfers between devices  112 us
    all_gather x1, waiting for transfers between devices, local(): piece = lax.all_gather(user_unit, 'batch', axis=0, tiled=True)  21.4 us
    all_to_all x1, blocking collectives, local(): lax.all_to_all(request, ('batch', 'item'), split_axis=0, concat_axis=0, t...  21.1 us
    all_to_all x1, waiting for transfers between devices, local(): lax.all_to_all(found, ('batch', 'item'), split_axis=0, concat_axis=0, til...  13.9 us
    all_to_all x1, waiting for transfers between devices, local(): lax.all_to_all(outgoing.reshape(devices, slots, width).astype(jnp.bfloat1...  12.9 us
    all_to_all x1, starting transfers between devices, local(): lax.all_to_all(outgoing.reshape(devices, slots, width).astype(jnp.bfloat1...  8.31 us
    scatter-add x1, other arithmetic, local(): jnp.zeros((item_table.shape[0], width), jnp.float32).at[asked.reshape(-1)]  7.29 us
    convert_element_type x1, other arithmetic, local(): return (table_grad.astype(jnp.bfloat16), weight_grad)  6 us
  transfers between devices with their start and end apart: 4, of which 4 were waited for; matrix products, arithmetic and copies ran while one was open for 7% of the time, Pallas kernels for 0%

commit v1 on v0

--- a/solution.py
+++ b/solution.py
@@ -6,6 +6,14 @@
 epsilon = 1e-06
 score_scale = 60.0
 cauchy_scale = 4.0
+
+
+def perform_columns(row_axis, here_x):
+    world_n = jax.lax.axis_size(row_axis)
+    ledger = tuple((world_n if kk == 0 else 1 for kk in range(here_x.ndim)))
+    return jax.lax.all_to_all(
+        jnp.tile(here_x, ledger), row_axis, tiled=True, split_axis=0, concat_axis=0
+    )
 
 
 def local(user_vectors, item_table, tower_weight, item_owner, item_row):
@@ -35,7 +43,7 @@
         * lax.rsqrt(jnp.mean(user_f * user_f, axis=1, keepdims=True) + epsilon)
         / jnp.sqrt(jnp.float32(width))
     ).astype(jnp.bfloat16)
-    piece = lax.all_gather(user_unit, "batch", axis=0, tiled=True)
+    piece = perform_columns("batch", user_unit)
     score = (
         lax.dot_general(
             item_vec, piece, (((1,), (1,)), ((), ())), preferred_element_type=jnp.float32

time: 246 us -> 248 us (level)
  blocking collectives: 21.1 us -> 50.3 us
  waiting for transfers between devices: 160 us -> 139 us
  starting transfers between devices: 12.7 us -> 8.78 us
    all_to_all x0 -> x1, blocking collectives: none -> 29.2 us  [perform_columns(): jax.lax.all_to_all(jnp.tile(here_x, ledger), row_axis, tiled=True, split_...]
    all_gather x1 -> x0, waiting for transfers between devices: 21.4 us -> none  [local(): piece = lax.all_gather(user_unit, 'batch', axis=0, tiled=True)]
    all_to_all x1, starting transfers between devices: 8.31 us -> 4.46 us  [local(): lax.all_to_all(outgoing.reshape(devices, slots, width).astype(jnp.bfloat1...]
    unnamed x3 -> x2, waiting for transfers between devices: 112 us -> 112 us
  transfers between devices with their start and end apart: 4 -> 3, of which waited for: 4 -> 3; matrix products, arithmetic and copies ran while one was open for 7% -> 7% of each run, Pallas kernels for 0% -> 0%
where the time goes in v1:
time: 248 us; the launch traced here: 247 us
  waiting for transfers between devices  139 us (56%)
  blocking collectives  50.3 us (20%)
  other arithmetic  16.6 us (7%)
  local copies, waits for them, and re-layouts  14.3 us (6%)
  between operations  14.2 us (6%)
  starting transfers between devices  8.78 us (4%)
  matrix products  3.74 us (2%)
    unnamed x2, waiting for transfers between devices  112 us
    all_to_all x1, blocking collectives, perform_columns(): jax.lax.all_to_all(jnp.tile(here_x, ledger), row_axis, tiled=True, split_...  29.2 us
    all_to_all x1, blocking collectives, local(): lax.all_to_all(request, ('batch', 'item'), split_axis=0, concat_axis=0, t...  21.1 us
    all_to_all x1, waiting for transfers between devices, local(): lax.all_to_all(found, ('batch', 'item'), split_axis=0, concat_axis=0, til...  13.9 us
    all_to_all x1, waiting for transfers between devices, local(): lax.all_to_all(outgoing.reshape(devices, slots, width).astype(jnp.bfloat1...  13 us
    scatter-add x1, other arithmetic, local(): jnp.zeros((item_table.shape[0], width), jnp.float32).at[asked.reshape(-1)]  7.29 us
    convert_element_type x1, other arithmetic, local(): return (table_grad.astype(jnp.bfloat16), weight_grad)  5.99 us
    gather x2, local copies, waits for them, and re-layouts, local(): found = item_table[asked]  5.63 us
  transfers between devices with their start and end apart: 3, of which 3 were waited for; matrix products, arithmetic and copies ran while one was open for 7% of the time, Pallas kernels for 0%

profile of v1, /device:TPU:1, one launch (start us, length us, event | category | flops | bytes accessed | tf_op | source)
XLA Modules:
  0.0 247.1 jit_solution(1646012434362527958)
XLA Ops:
  7.2 0.0 copy-start
  7.2 0.8 copy.10
  8.0 0.2 fusion.12
  8.3 0.9 fusion.13
  9.2 0.7 compare_select_fusion.2
  9.9 1.6 scatter_custom_fusion
  11.4 0.1 all_to_all.20
  11.6 21.1 %all_to_all.31 = s32[128,1,4]{2,1,0:T(1,128)S(1)} all-to-all(s32[128,1,4]{2,1,0:T(1,128)S(1)} %bitcast.37), channel_id=1, replica_groups=mesh['batch'=8,'item'=16] {'batch','item'}, dimensions={0} | all-to-all | bytes 4096 | tf_op jit(solution)/shard_map/all_to_all | solution.py:32
  32.7 0.1 reshape.154
  32.8 4.7 %gather_fusion = bf16[512,512]{1,0:T(8,128)(2,1)S(1)} fusion(bf16[4096,512]{1,0:T(8,128)(2,1)} %param.6, s32[1024]{0:T(1024)S(1)} %pad_clamp_fusion.1), kind=kCustom, calls=%fused_computation | custom fusion | bytes 1050624 | tf_op jit(solution)/shard_map/gather | solution.py:33
  37.5 0.0 copy-start.1
  37.5 0.9 reshape.153
  38.4 4.3 %all-to-all-start.1 = ((bf16[128,4,512]{2,1,0:T(4,128)(2,1)}), bf16[128,4,512]{2,1,0:T(4,128)(2,1)S(1)}, u32[]{:S(2)}, u32[]{:S(2)}) async-start(bf16[128,4,512]{2,1,0:T(4,128)(2,1)} %reshape.153), calls=%async_computation.1 | async-start | bytes 1048576 | tf_op jit(solution)/shard_map/all_to_all | solution.py:34
  42.7 0.0 all-reduce.3.cloned.1.call-start
  42.8 0.0 copy-done.1
  42.8 0.1 fusion.6
  42.9 13.9 %all-to-all-done.1 = bf16[128,4,512]{2,1,0:T(4,128)(2,1)S(1)} async-done(((bf16[128,4,512]{2,1,0:T(4,128)(2,1)}), bf16[128,4,512]{2,1,0:T(4,128)(2,1)S(1)}, u32[]{:S(2)}, u32[]{:S(2)}) %all-to-all-start.1) | async-done | bytes 524320 | tf_op jit(solution)/shard_map/all_to_all | solution.py:34
  56.8 0.1 reshape.147
  57.0 1.2 gather_fusion.1
  58.1 0.0 copy-done
  58.1 0.4 multiply_reduce_fusion.1
  58.5 0.3 fusion.9
  58.8 0.2 tile.2
  59.0 29.2 %all_to_all.32 = bf16[8,256,512]{2,1,0:T(8,128)(2,1)S(1)} all-to-all(bf16[8,256,512]{2,1,0:T(8,128)(2,1)S(1)} %tile.2), channel_id=1, replica_groups=mesh['batch'=8,'item'=16] {'batch'}, dimensions={0} | all-to-all | bytes 4194304 | tf_op jit(solution)/shard_map/all_to_all | solution.py:14
  88.2 0.9 fusion.19
  89.1 0.9 multiply_reduce_fusion
  89.9 0.2 multiply_convert_fusion
  90.1 1.3 fusion.21
  91.4 0.0 all-reduce.3.cloned.1.call-update
  91.5 0.3 fusion.20
  91.8 1.7 scatter_custom_fusion.1
  93.5 0.1 convert_element_type.44
  93.6 0.9 convert_element_type.45
  94.5 4.5 %all-to-all-start.3 = ((bf16[128,4,512]{2,1,0:T(4,128)(2,1)}), bf16[128,4,512]{2,1,0:T(4,128)(2,1)S(1)}, u32[]{:S(2)}, u32[]{:S(2)}) async-start(bf16[128,4,512]{2,1,0:T(4,128)(2,1)} %convert_element_type.45), calls=%async_computation.3 | async-start | bytes 1048576 | tf_op jit(solution)/shard_map/all_to_all | solution.py:75
  98.9 0.5 broadcast.188
  99.5 0.8 reduce.3
  100.3 0.1 reshape.146
  100.4 13.0 %all-to-all-done.3 = bf16[128,4,512]{2,1,0:T(4,128)(2,1)S(1)} async-done(((bf16[128,4,512]{2,1,0:T(4,128)(2,1)}), bf16[128,4,512]{2,1,0:T(4,128)(2,1)S(1)}, u32[]{:S(2)}, u32[]{:S(2)}) %all-to-all-start.3) | async-done | bytes 524320 | tf_op jit(solution)/shard_map/all_to_all | solution.py:75
  113.4 0.1 reshape.188
  113.5 7.3 %scatter_custom_fusion.2 = f32[4096,512]{1,0:T(8,128)} fusion(s32[512]{0:T(512)S(1)} %bitcast.45, f32[512,512]{1,0:T(8,128)S(1)} %reshape.188, f32[]{:T(128)} %constant.12.clone.1), kind=kCustom, calls=%fused_computation.5 | custom fusion | flops 262144 | bytes 8388612 | tf_op jit(solution)/shard_map/scatter-add | solution.py:84
  120.7 6.0 %convert_element_type.46 = bf16[4096,512]{1,0:T(8,128)(2,1)} convert(f32[4096,512]{1,0:T(8,128)} %scatter_custom_fusion.2) | non-fusion elementwise | flops 2097152 | bytes 12582912 | tf_op jit(solution)/shard_map/convert_element_type | solution.py:86
  126.7 112.2 %all-reduce.3.cloned.1.call-done = f32[512,512]{1,0:T(8,128)} async-done(((f32[512,512]{1,0:T(8,128)}), f32[512,512]{1,0:T(8,128)}) %all-reduce.3.cloned.1.call-update) | async-done | bytes 1048592
  239.0 1.3 constant_dynamic-slice_fusion
  (13 shorter events, 0.1 us)
Async XLA Ops:
  7.2 50.9 %copy-start = (bf16[512,512]{1,0:T(8,128)(2,1)S(1)}, bf16[512,512]{1,0:T(8,128)(2,1)}, u32[]{:S(2)}) copy-start(bf16[512,512]{1,0:T(8,128)(2,1)} %param.7) | copy-start | bytes 1572868
  37.5 5.3 %copy-start.1 = (bf16[256,512]{1,0:T(8,128)(2,1)S(1)}, bf16[256,512]{1,0:T(8,128)(2,1)}, u32[]{:S(2)}) copy-start(bf16[256,512]{1,0:T(8,128)(2,1)} %param.5) | copy-start | bytes 786436
  38.4 18.4 %all-to-all-start.1 = ((bf16[128,4,512]{2,1,0:T(4,128)(2,1)}), bf16[128,4,512]{2,1,0:T(4,128)(2,1)S(1)}, u32[]{:S(2)}, u32[]{:S(2)}) async-start(bf16[128,4,512]{2,1,0:T(4,128)(2,1)} %reshape.153), calls=%async_computation.1 | async-start | bytes 1048576 | tf_op jit(solution)/shard_map/all_to_all | solution.py:34
  42.7 196.3 %all-reduce.3.cloned.1.call-start = ((), (), s32[]{:S(2)}) async-start(), calls=%async_computation.4 | async-start | bytes 2097152
  94.5 18.9 %all-to-all-start.3 = ((bf16[128,4,512]{2,1,0:T(4,128)(2,1)}), bf16[128,4,512]{2,1,0:T(4,128)(2,1)S(1)}, u32[]{:S(2)}, u32[]{:S(2)}) async-start(bf16[128,4,512]{2,1,0:T(4,128)(2,1)} %convert_element_type.45), calls=%async_computation.3 | async-start | bytes 1048576 | tf_op jit(solution)/shard_map/all_to_all | solution.py:75
Sparse Core Ops, SparseCore 0:
  91.6 147.3 all-reduce.2
